TPU v7x, 32 devices: a whole 2x2x4 slice. The times are simulated.
32 devices in a mesh: sec: 2 (over core), row: 4 (over y, x), col: 4 (over z).
Axes of the slice: x: 2, y: 2, z: 4, core: 2. Of those that a mesh axis runs over, the one named last changes fastest.
Arguments:
- anc_inverse: float32 [2048, 2048], P('row', ('sec', 'col')), as said below
- panel: float32 [8192, 2048], P(('sec', 'col'), 'row'), may hold values from -0.5 to 0.5
- diag_inverse: float32 [8192, 512], P(('sec', 'col')), may hold values from -6 to 6
- widths: int32 [16], replicated, may hold values from 1 to 4, as said below
- pattern: int32 [16, 16], replicated, may hold values 0 or 1
Outputs:
- off_inverse: float32 [8192, 2048], P(('sec', 'col'), 'row')
- child_inverse: float32 [8192, 512], P(('sec', 'col'))
Inputs may be any that keep to these rules, and one draw needn't show every extreme that they name: `anc_inverse`: exactly symmetric. `widths`: both 1 and 4 occur in every draw.
All inputs are finite; a program needn't handle non-finite values.
Results may differ from a plain program's by a relative error of at most 0.0003.
Values sent between devices are 32-bit elements; how exact they have to be, the bound alone decides.
A program may use at most 128 MiB of HBM per device.

v0:
```python
import jax
import jax.numpy as jnp
from jax import lax
from jax.sharding import PartitionSpec as P

B = 128
SW = 512


def mask_rows(values, slot_count, column_mask, block_mask, offset):
    amount = values.shape[1]
    window = lax.dynamic_slice_in_dim(block_mask, offset, amount, 1)
    shaped = (
        values.reshape(slot_count, SW, amount)
        * column_mask.reshape(slot_count, SW, 1)
        * window[:, None, :]
    )
    return shaped.reshape(slot_count * SW, amount)


def local(anc_inverse, panel, diag_inverse, widths, pattern):
    highest = lax.Precision.HIGHEST
    local_rows, rows_here = panel.shape
    slot_count = local_rows // SW
    slot_first = (lax.axis_index("sec") * lax.axis_size("col") + lax.axis_index("col")) * slot_count
    row_offset = lax.axis_index("row") * rows_here
    my_widths = lax.dynamic_slice_in_dim(widths, slot_first, slot_count)
    my_pattern = lax.dynamic_slice_in_dim(pattern, slot_first, slot_count, 0)
    block_mask = jnp.repeat(my_pattern.astype(jnp.float32), B, axis=1)
    position = jnp.arange(SW, dtype=jnp.int32)
    column_mask = (position[None, :] < my_widths[:, None] * B).astype(jnp.float32)
    anc_rows = lax.all_gather(anc_inverse, ("sec", "col"), axis=1, tiled=True)
    local_panel = mask_rows(panel, slot_count, column_mask, block_mask, row_offset)
    product = lax.psum_scatter(
        lax.dot_general(
            anc_rows,
            local_panel,
            (((0,), (1,)), ((), ())),
            precision=highest,
            preferred_element_type=jnp.float32,
        ),
        "row",
        scatter_dimension=0,
        tiled=True,
    ).T
    product = mask_rows(product, slot_count, column_mask, block_mask, row_offset)
    update = jnp.einsum(
        "jai,jbi->jab",
        product.reshape(slot_count, SW, rows_here),
        local_panel.reshape(slot_count, SW, rows_here),
        precision=highest,
    )
    summed = lax.psum(update.reshape(local_rows, SW), "row")
    pair_mask = column_mask[:, :, None] * column_mask[:, None, :]
    diag_block = (diag_inverse + summed) * pair_mask.reshape(local_rows, SW)
    return (-product, diag_block)


def solution(mesh):
    in_specs = (
        P("row", ("sec", "col")),
        P(("sec", "col"), "row"),
        P(("sec", "col"), None),
        P(),
        P(),
    )
    out_specs = (P(("sec", "col"), "row"), P(("sec", "col"), None))
    return jax.shard_map(local, mesh=mesh, in_specs=in_specs, out_specs=out_specs, check_vma=False)
```

profile of v0, /device:TPU:0, one launch (start us, length us, event | category | flops | bytes accessed | tf_op | source)
XLA Modules:
  0.0 249.4 jit_solution(4259381773065099106)
XLA Ops:
  7.2 0.0 all-gather.2.cloned.1.call-start
  7.2 0.7 all-gather.2.cloned.1.call-update
  7.9 0.0 reduce-scatter.2.cloned.1.call-start
  8.0 0.7 dynamic-slice_multiply_fusion
  8.7 0.1 compare_convert_fusion
  8.8 0.7 dynamic-slice_convert_fusion
  9.5 0.1 broadcast_bitcast_fusion
  9.6 1.8 bitcast_multiply_fusion.1
  11.4 47.8 %all-gather.2.cloned.1.call-done = f32[512,2048]{1,0:T(8,128)} async-done(((f32[512,256]{1,0:T(8,128)}), f32[512,2048]{1,0:T(8,128)}) %all-gather.2.cloned.1.call-update) | async-done | bytes 4194320 | tf_op jit(solution)/shard_map/all_gather | solution.py:32
  59.2 17.3 %convolution_bitcast_fusion = f32[2048,1024]{0,1:T(8,128)} fusion(f32[1024,512]{1,0:T(8,128)S(1)} %bitcast_multiply_fusion.1, f32[512,2048]{1,0:T(8,128)} %all-gather.2.cloned.1.call-done), kind=kOutput, calls=%fused_computation | convolution fusion | flops 12884901888 | bytes 14680064 | tf_op jit(solution)/shard_map/dot_general | solution.py:35
  76.5 0.0 copy-start
  76.5 0.0 reduce-scatter.2.cloned.1.call-update
  76.5 0.0 all-reduce.2.cloned.1.call-start
  76.6 85.2 %reduce-scatter.2.cloned.1.call-done = f32[512,1024]{0,1:T(8,128)} async-done(((f32[2048,1024]{0,1:T(8,128)}), f32[512,1024]{0,1:T(8,128)}) %reduce-scatter.2.cloned.1.call-update) | async-done | bytes 2097168 | tf_op jit(solution)/shard_map/reduce_scatter | solution.py:34
  161.8 0.0 copy-done
  161.8 6.7 %fusion.2 = f32[2,512,512]{2,1,0:T(8,128)} fusion(f32[2,512,512]{2,1,0:T(8,128)S(1)} %bitcast.29, f32[2,512,512]{2,1,0:T(8,128)} %bitcast.31, f32[2,512]{1,0:T(2,128)S(1)} %get-tuple-element.4, f32[2,512]{1,0:T(2,128)S(1)} %constant_dynamic-slice_fusion), kind=kOutput, calls=%fused_computation.7 | convolution fusion | flops 3223322624 | bytes 6299648 | tf_op jit(solution)/shard_map/jai,jbi->jab/dot_general | solution.py:47
  168.5 0.0 copy-start.1
  168.5 0.0 all-reduce.2.cloned.1.call-update
  168.6 69.7 %all-reduce.2.cloned.1.call-done = f32[1024,512]{1,0:T(8,128)} async-done(((f32[1024,512]{1,0:T(8,128)}), f32[1024,512]{1,0:T(8,128)}) %all-reduce.2.cloned.1.call-update) | async-done | bytes 2097168 | tf_op jit(solution)/shard_map/psum | solution.py:53
  238.2 0.0 copy-done.1
  238.2 4.7 %fusion.1 = (f32[1024,512]{1,0:T(8,128)}, f32[1024,512]{1,0:T(8,128)}) fusion(f32[1024,512]{1,0:T(8,128)} %param.7, f32[1024,512]{1,0:T(8,128)} %all-reduce.2.cloned.1.call-done, f32[2,512]{1,0:T(2,128)S(1)} %get-tuple-element.4, f32[1024]{0:T(1024)S(1)} %bitcast.33, f32[2,512]{1,0:T(2,128)S(1)} %constant_dynamic-slice_fusion, f32[512,1024]{0,1:T(8,128)S(1)} %copy-done.1), kind=kLoop, calls=%fused_computation.5 | loop fusion | flops 3145728 | bytes 10498048 | tf_op jit(solution)/shard_map/mul | solution.py:55
  (3 shorter events, 0.0 us)
Async XLA Ops:
  7.2 52.0 %all-gather.2.cloned.1.call-start = ((), (), s32[]{:S(2)}) async-start(), calls=%async_computation.1 | async-start | bytes 4718592 | tf_op jit(solution)/shard_map/all_gather | solution.py:32
  7.9 153.9 %reduce-scatter.2.cloned.1.call-start = ((), (), s32[]{:S(2)}) async-start(), calls=%async_computation.2 | async-start | bytes 10485760 | tf_op jit(solution)/shard_map/reduce_scatter | solution.py:34
  76.5 85.3 %copy-start = (f32[1024,512]{1,0:T(8,128)S(1)}, f32[1024,512]{1,0:T(8,128)}, u32[]{:S(2)}) copy-start(f32[1024,512]{1,0:T(8,128)} %param.6) | copy-start | bytes 6291460
  76.5 161.7 %all-reduce.2.cloned.1.call-start = ((), (), s32[]{:S(2)}) async-start(), calls=%async_computation.3 | async-start | bytes 4194304 | tf_op jit(solution)/shard_map/psum | solution.py:53
  168.5 69.7 %copy-start.1 = (f32[512,1024]{0,1:T(8,128)S(1)}, f32[512,1024]{0,1:T(8,128)}, u32[]{:S(2)}) copy-start(f32[512,1024]{0,1:T(8,128)} %reduce-scatter.2.cloned.1.call-done) | copy-start | bytes 6291460
Sparse Core Ops, SparseCore 0:
  9.6 49.5 all-gather.1
  76.6 85.1 reduce-scatter.1
  168.7 69.4 all-reduce.1
where the time goes:
time: 250 us; the launch traced here: 249 us
  waiting for transfers between devices  203 us (81%)
  matrix products  24 us (10%)
  between operations  13.8 us (6%)
  other arithmetic  8.03 us (3%)
    reduce_scatter x1, waiting for transfers between devices, local(): lax.psum_scatter(lax.dot_general(anc_rows, local_panel, (((0,), (1,)), ((...  85.2 us
    psum x1, waiting for transfers between devices, local(): summed = lax.psum(update.reshape(local_rows, SW), 'row')  69.7 us
    all_gather x1, waiting for transfers between devices, local(): anc_rows = lax.all_gather(anc_inverse, ('sec', 'col'), axis=1, tiled=True)  47.8 us
    dot_general x1, matrix products, local(): lax.dot_general(anc_rows, local_panel, (((0,), (1,)), ((), ())), precisio...  17.3 us
    dot_general x1, matrix products, local(): jnp.einsum('jai,jbi->jab', product.reshape(slot_count, SW, rows_here), lo...  6.73 us
  transfers between devices with their start and end apart: 3, of which 3 were waited for; matrix products, arithmetic and copies ran while one was open for 1% of the time, Pallas kernels for 0%

commit v1 on v0

--- a/solution.py
+++ b/solution.py
@@ -29,7 +29,12 @@
     block_mask = jnp.repeat(my_pattern.astype(jnp.float32), B, axis=1)
     position = jnp.arange(SW, dtype=jnp.int32)
     column_mask = (position[None, :] < my_widths[:, None] * B).astype(jnp.float32)
-    anc_rows = lax.all_gather(anc_inverse, ("sec", "col"), axis=1, tiled=True)
+    anc_rows = jnp.concatenate(
+        lax.all_to_all(
+            jnp.stack([anc_inverse] * lax.axis_size(("sec", "col"))), ("sec", "col"), 0, 0
+        ),
+        axis=1,
+    )
     local_panel = mask_rows(panel, slot_count, column_mask, block_mask, row_offset)
     product = lax.psum_scatter(
         lax.dot_general(

time: 250 us -> 302 us (1.21)
  waiting for transfers between devices: 203 us -> 245 us
  starting transfers between devices: 0.12 us -> 6.74 us
  local copies, waits for them, and re-layouts: 0.11 us -> 3.83 us
    all_to_all x0 -> x1, waiting for transfers between devices: none -> 90.6 us  [local(): lax.all_to_all(jnp.stack([anc_inverse] * lax.axis_size(('sec', 'col'))),...]
    all_gather x1 -> x0, waiting for transfers between devices: 47.8 us -> none  [local(): anc_rows = lax.all_gather(anc_inverse, ('sec', 'col'), axis=1, tiled=True)]
    all_to_all x0 -> x1, starting transfers between devices: none -> 6.49 us  [local(): lax.all_to_all(jnp.stack([anc_inverse] * lax.axis_size(('sec', 'col'))),...]
where the time goes in v1:
time: 302 us; the launch traced here: 301 us
  waiting for transfers between devices  245 us (81%)
  matrix products  24.1 us (8%)
  between operations  14.1 us (5%)
  other arithmetic  7.38 us (2%)
  starting transfers between devices  6.74 us (2%)
  local copies, waits for them, and re-layouts  3.83 us (1%)
    all_to_all x1, waiting for transfers between devices, local(): lax.all_to_all(jnp.stack([anc_inverse] * lax.axis_size(('sec', 'col'))),...  90.6 us
    reduce_scatter x1, waiting for transfers between devices, local(): lax.psum_scatter(lax.dot_general(anc_rows, local_panel, (((0,), (1,)), ((...  84.9 us
    psum x1, waiting for transfers between devices, local(): summed = lax.psum(update.reshape(local_rows, SW), 'row')  69.6 us
    dot_general x1, matrix products, local(): lax.dot_general(anc_rows, local_panel, (((0,), (1,)), ((), ())), precisio...  17.3 us
    dot_general x1, matrix products, local(): jnp.einsum('jai,jbi->jab', product.reshape(slot_count, SW, rows_here), lo...  6.73 us
    all_to_all x1, starting transfers between devices, local(): lax.all_to_all(jnp.stack([anc_inverse] * lax.axis_size(('sec', 'col'))),...  6.49 us
  transfers between devices with their start and end apart: 3, of which 3 were waited for; matrix products, arithmetic and copies ran while one was open for 1% of the time, Pallas kernels for 0%

profile of v1, /device:TPU:0, one launch (start us, length us, event | category | flops | bytes accessed | tf_op | source)
XLA Modules:
  0.0 301.3 jit_solution(16830383895719228144)
XLA Ops:
  7.2 1.2 copy.7
  8.4 2.5 stack.2
  10.9 0.0 copy-start.2
  10.9 6.5 %all-to-all-start = ((f32[8,512,256]{1,2,0:T(8,128)}), f32[8,512,256]{1,2,0:T(8,128)}, u32[]{:S(2)}, u32[]{:S(2)}) async-start(f32[8,512,256]{1,2,0:T(8,128)} %stack.2), calls=%async_computation | async-start | bytes 8388608 | tf_op jit(solution)/shard_map/all_to_all | solution.py:33
  17.4 0.0 reduce-scatter.2.cloned.1.call-start
  17.4 0.0 copy-done.2
  17.4 0.1 dynamic-slice_multiply_fusion
  17.5 0.1 compare_convert_fusion
  17.6 0.7 dynamic-slice_convert_fusion
  18.3 0.1 broadcast_bitcast_fusion
  18.4 1.8 bitcast_multiply_fusion.1
  20.2 90.6 %all-to-all-done = f32[8,512,256]{1,2,0:T(8,128)} async-done(((f32[8,512,256]{1,2,0:T(8,128)}), f32[8,512,256]{1,2,0:T(8,128)}, u32[]{:S(2)}, u32[]{:S(2)}) %all-to-all-start) | async-done | bytes 4194336 | tf_op jit(solution)/shard_map/all_to_all | solution.py:33
  110.9 17.3 %convolution_bitcast_fusion = f32[2048,1024]{0,1:T(8,128)} fusion(f32[1024,512]{1,0:T(8,128)S(1)} %bitcast_multiply_fusion.1, f32[512,2048]{0,1:T(8,128)} %bitcast.2), kind=kOutput, calls=%fused_computation | convolution fusion | flops 12884901888 | bytes 14680064 | tf_op jit(solution)/shard_map/dot_general | solution.py:40
  128.2 0.0 copy-start
  128.2 0.0 reduce-scatter.2.cloned.1.call-update
  128.2 0.2 all-reduce.2.cloned.1.call-start
  128.5 84.9 %reduce-scatter.2.cloned.1.call-done = f32[512,1024]{0,1:T(8,128)} async-done(((f32[2048,1024]{0,1:T(8,128)}), f32[512,1024]{0,1:T(8,128)}) %reduce-scatter.2.cloned.1.call-update) | async-done | bytes 2097168 | tf_op jit(solution)/shard_map/reduce_scatter | solution.py:39
  213.4 0.0 copy-done
  213.4 6.7 %fusion.2 = f32[2,512,512]{2,1,0:T(8,128)} fusion(f32[2,512,512]{2,1,0:T(8,128)S(1)} %bitcast.32, f32[2,512,512]{2,1,0:T(8,128)} %bitcast.34, f32[2,512]{1,0:T(2,128)S(1)} %get-tuple-element.4, f32[2,512]{1,0:T(2,128)S(1)} %constant_dynamic-slice_fusion), kind=kOutput, calls=%fused_computation.7 | convolution fusion | flops 3223322624 | bytes 6299648 | tf_op jit(solution)/shard_map/jai,jbi->jab/dot_general | solution.py:52
  220.1 0.0 copy-start.1
  220.1 0.0 all-reduce.2.cloned.1.call-update
  220.1 69.6 %all-reduce.2.cloned.1.call-done = f32[1024,512]{1,0:T(8,128)} async-done(((f32[1024,512]{1,0:T(8,128)}), f32[1024,512]{1,0:T(8,128)}) %all-reduce.2.cloned.1.call-update) | async-done | bytes 2097168 | tf_op jit(solution)/shard_map/psum | solution.py:58
  289.7 0.0 copy-done.1
  289.7 4.7 %fusion.1 = (f32[1024,512]{1,0:T(8,128)}, f32[1024,512]{1,0:T(8,128)}) fusion(f32[1024,512]{1,0:T(8,128)} %param.7, f32[1024,512]{1,0:T(8,128)} %all-reduce.2.cloned.1.call-done, f32[2,512]{1,0:T(2,128)S(1)} %get-tuple-element.4, f32[1024]{0:T(1024)S(1)} %bitcast.36, f32[2,512]{1,0:T(2,128)S(1)} %constant_dynamic-slice_fusion, f32[512,1024]{0,1:T(8,128)S(1)} %copy-done.1), kind=kLoop, calls=%fused_computation.5 | loop fusion | flops 3145728 | bytes 10498048 | tf_op jit(solution)/shard_map/mul | solution.py:60
  (3 shorter events, 0.0 us)
Async XLA Ops:
  10.9 6.5 %copy-start.2 = (s32[16]{0:T(128)S(1)}, s32[16]{0:T(128)}, u32[]{:S(2)}) copy-start(s32[16]{0:T(128)} %param.8) | copy-start | bytes 196
  10.9 100.0 %all-to-all-start = ((f32[8,512,256]{1,2,0:T(8,128)}), f32[8,512,256]{1,2,0:T(8,128)}, u32[]{:S(2)}, u32[]{:S(2)}) async-start(f32[8,512,256]{1,2,0:T(8,128)} %stack.2), calls=%async_computation | async-start | bytes 8388608 | tf_op jit(solution)/shard_map/all_to_all | solution.py:33
  17.4 196.0 %reduce-scatter.2.cloned.1.call-start = ((), (), s32[]{:S(2)}) async-start(), calls=%async_computation.2 | async-start | bytes 10485760 | tf_op jit(solution)/shard_map/reduce_scatter | solution.py:39
  128.2 85.2 %copy-start = (f32[1024,512]{1,0:T(8,128)S(1)}, f32[1024,512]{1,0:T(8,128)}, u32[]{:S(2)}) copy-start(f32[1024,512]{1,0:T(8,128)} %param.6) | copy-start | bytes 6291460
  128.2 161.5 %all-reduce.2.cloned.1.call-start = ((), (), s32[]{:S(2)}) async-start(), calls=%async_computation.3 | async-start | bytes 4194304 | tf_op jit(solution)/shard_map/psum | solution.py:58
  220.1 69.6 %copy-start.1 = (f32[512,1024]{0,1:T(8,128)S(1)}, f32[512,1024]{0,1:T(8,128)}, u32[]{:S(2)}) copy-start(f32[512,1024]{0,1:T(8,128)} %reduce-scatter.2.cloned.1.call-done) | copy-start | bytes 6291460
Sparse Core Ops, SparseCore 0:
  128.4 84.9 reduce-scatter.1
  220.2 69.4 all-reduce.1

commit v2 on v0

--- a/solution.py
+++ b/solution.py
@@ -50,7 +50,7 @@
         local_panel.reshape(slot_count, SW, rows_here),
         precision=highest,
     )
-    summed = lax.psum(update.reshape(local_rows, SW), "row")
+    summed = jnp.sum(lax.all_gather(update.reshape(local_rows, SW), "row"), axis=0)
     pair_mask = column_mask[:, :, None] * column_mask[:, None, :]
     diag_block = (diag_inverse + summed) * pair_mask.reshape(local_rows, SW)
     return (-product, diag_block)

time: 250 us -> 274 us (1.096)
  waiting for transfers between devices: 203 us -> 221 us
  other arithmetic: 8.03 us -> 14 us
    all_gather x0 -> x1, waiting for transfers between devices: none -> 87.6 us  [local(): lax.all_gather(update.reshape(local_rows, SW), 'row')]
    psum x1 -> x0, waiting for transfers between devices: 69.7 us -> none  [local(): summed = lax.psum(update.reshape(local_rows, SW), 'row')]
    reduce_sum x0 -> x1, other arithmetic: none -> 5.95 us  [local(): jnp.sum(lax.all_gather(update.reshape(local_rows, SW), 'row'), axis=0)]
where the time goes in v2:
time: 274 us; the launch traced here: 273 us
  waiting for transfers between devices  221 us (81%)
  matrix products  24 us (9%)
  other arithmetic  14 us (5%)
  between operations  13.8 us (5%)
    all_gather x1, waiting for transfers between devices, local(): lax.all_gather(update.reshape(local_rows, SW), 'row')  87.6 us
    reduce_scatter x1, waiting for transfers between devices, local(): lax.psum_scatter(lax.dot_general(anc_rows, local_panel, (((0,), (1,)), ((...  85 us
    all_gather x1, waiting for transfers between devices, local(): anc_rows = lax.all_gather(anc_inverse, ('sec', 'col'), axis=1, tiled=True)  47.8 us
    dot_general x1, matrix products, local(): lax.dot_general(anc_rows, local_panel, (((0,), (1,)), ((), ())), precisio...  17.3 us
    dot_general x1, matrix products, local(): jnp.einsum('jai,jbi->jab', product.reshape(slot_count, SW, rows_here), lo...  6.73 us
    reduce_sum x1, other arithmetic, local(): jnp.sum(lax.all_gather(update.reshape(local_rows, SW), 'row'), axis=0)  5.95 us
  transfers between devices with their start and end apart: 3, of which 3 were waited for; matrix products, arithmetic and copies ran while one was open for 1% of the time, Pallas kernels for 0%

profile of v2, /device:TPU:0, one launch (start us, length us, event | category | flops | bytes accessed | tf_op | source)
XLA Modules:
  0.0 273.4 jit_solution(8294116059753729394)
XLA Ops:
  7.2 0.0 all-gather.3.cloned.1.call-start
  7.2 0.7 all-gather.3.cloned.1.call-update
  7.9 0.0 reduce-scatter.2.cloned.1.call-start
  8.0 0.7 dynamic-slice_multiply_fusion
  8.7 0.1 compare_convert_fusion
  8.8 0.7 dynamic-slice_convert_fusion
  9.5 0.1 broadcast_bitcast_fusion
  9.6 1.8 bitcast_multiply_fusion.1
  11.4 47.8 %all-gather.3.cloned.1.call-done = f32[512,2048]{1,0:T(8,128)} async-done(((f32[512,256]{1,0:T(8,128)}), f32[512,2048]{1,0:T(8,128)}) %all-gather.3.cloned.1.call-update) | async-done | bytes 4194320 | tf_op jit(solution)/shard_map/all_gather | solution.py:32
  59.2 17.3 %convolution_bitcast_fusion = f32[2048,1024]{0,1:T(8,128)} fusion(f32[1024,512]{1,0:T(8,128)S(1)} %bitcast_multiply_fusion.1, f32[512,2048]{1,0:T(8,128)} %all-gather.3.cloned.1.call-done), kind=kOutput, calls=%fused_computation | convolution fusion | flops 12884901888 | bytes 14680064 | tf_op jit(solution)/shard_map/dot_general | solution.py:35
  76.5 0.0 copy-start
  76.5 0.0 reduce-scatter.2.cloned.1.call-update
  76.5 0.2 all-gather.5.cloned.1.call-start
  76.8 85.0 %reduce-scatter.2.cloned.1.call-done = f32[512,1024]{0,1:T(8,128)} async-done(((f32[2048,1024]{0,1:T(8,128)}), f32[512,1024]{0,1:T(8,128)}) %reduce-scatter.2.cloned.1.call-update) | async-done | bytes 2097168 | tf_op jit(solution)/shard_map/reduce_scatter | solution.py:34
  161.8 0.0 copy-done
  161.8 6.7 %fusion.2 = f32[2,512,512]{2,1,0:T(8,128)} fusion(f32[2,512,512]{2,1,0:T(8,128)S(1)} %bitcast.29, f32[2,512,512]{2,1,0:T(8,128)} %bitcast.31, f32[2,512]{1,0:T(2,128)S(1)} %get-tuple-element.4, f32[2,512]{1,0:T(2,128)S(1)} %constant_dynamic-slice_fusion), kind=kOutput, calls=%fused_computation.7 | convolution fusion | flops 3223322624 | bytes 6299648 | tf_op jit(solution)/shard_map/jai,jbi->jab/dot_general | solution.py:47
  168.5 0.0 all-gather.5.cloned.1.call-update
  168.6 0.0 copy-start.1
  168.6 87.6 %all-gather.5.cloned.1.call-done = f32[4,1024,512]{2,1,0:T(8,128)} async-done(((f32[1,1024,512]{2,1,0:T(8,128)}), f32[4,1024,512]{2,1,0:T(8,128)}) %all-gather.5.cloned.1.call-update) | async-done | bytes 8388624 | tf_op jit(solution)/shard_map/all_gather | solution.py:53
  256.2 6.0 %reduce_sum.9 = f32[1024,512]{1,0:T(8,128)} reduce(f32[4,1024,512]{2,1,0:T(8,128)} %all-gather.5.cloned.1.call-done, f32[]{:T(128)} %constant.28.clone.1), dimensions={0}, to_apply=%region_1.0 | reduce | flops 1572864 | bytes 10485764 | tf_op jit(solution)/shard_map/reduce_sum | solution.py:53
  262.2 0.0 copy-done.1
  262.2 4.7 %fusion.1 = (f32[1024,512]{1,0:T(8,128)}, f32[1024,512]{1,0:T(8,128)}) fusion(f32[1024,512]{1,0:T(8,128)} %param.7, f32[1024,512]{1,0:T(8,128)} %reduce_sum.9, f32[2,512]{1,0:T(2,128)S(1)} %get-tuple-element.4, f32[1024]{0:T(1024)S(1)} %bitcast.33, f32[2,512]{1,0:T(2,128)S(1)} %constant_dynamic-slice_fusion, f32[512,1024]{0,1:T(8,128)S(1)} %copy-done.1), kind=kLoop, calls=%fused_computation.5 | loop fusion | flops 3145728 | bytes 10498048 | tf_op jit(solution)/shard_map/mul | solution.py:55
  (3 shorter events, 0.0 us)
Async XLA Ops:
  7.2 52.0 %all-gather.3.cloned.1.call-start = ((), (), s32[]{:S(2)}) async-start(), calls=%async_computation.1 | async-start | bytes 4718592 | tf_op jit(solution)/shard_map/all_gather | solution.py:32
  7.9 153.9 %reduce-scatter.2.cloned.1.call-start = ((), (), s32[]{:S(2)}) async-start(), calls=%async_computation.2 | async-start | bytes 10485760 | tf_op jit(solution)/shard_map/reduce_scatter | solution.py:34
  76.5 85.3 %copy-start = (f32[1024,512]{1,0:T(8,128)S(1)}, f32[1024,512]{1,0:T(8,128)}, u32[]{:S(2)}) copy-start(f32[1024,512]{1,0:T(8,128)} %param.6) | copy-start | bytes 6291460
  76.5 179.7 %all-gather.5.cloned.1.call-start = ((), (), s32[]{:S(2)}) async-start(), calls=%async_computation.3 | async-start | bytes 10485760 | tf_op jit(solution)/shard_map/all_gather | solution.py:53
  168.6 93.6 %copy-start.1 = (f32[512,1024]{0,1:T(8,128)S(1)}, f32[512,1024]{0,1:T(8,128)}, u32[]{:S(2)}) copy-start(f32[512,1024]{0,1:T(8,128)} %reduce-scatter.2.cloned.1.call-done) | copy-start | bytes 6291460
Sparse Core Ops, SparseCore 0:
  9.6 49.5 all-gather.2
  76.6 85.1 reduce-scatter.1
  168.7 87.4 all-gather.4
